TPU v7x, 256 devices: a whole 4x4x8 slice. The times are simulated.
256 devices in a mesh: head: 16 (over x, y), qblk: 16 (over z, core).
Axes of the slice: x: 4, y: 4, z: 8, core: 2. Of those that a mesh axis runs over, the one named last changes fastest.
Arguments:
- queries: bfloat16 [32768, 4096], P(('qblk', 'head')), may hold values from -6 to 6
- key_states: bfloat16 [32768, 1024], P(('qblk', 'head')), may hold values from -6 to 6
- value_states: bfloat16 [32768, 1024], P(('qblk', 'head')), may hold values from -6 to 6
- vertical_blocks: int32 [32, 5], replicated, may hold values from 0 to 510, as said below
- slash_offsets: int32 [32, 8], replicated, may hold values from 1 to 64, as said below
Outputs:
- attended: bfloat16 [32768, 4096], P(('qblk', 'head'))
Inputs may be any that keep to these rules, and one draw needn't show every extreme that they name: `vertical_blocks`: each head names 5 distinct blocks, among them block 0 and block 510. `slash_offsets`: each head names 8 distinct offsets, among them 1 and 64.
All inputs are finite; a program needn't handle non-finite values.
Results may differ from a plain program's by a relative error of at most 0.0033.
Values may be sent and summed in bfloat16 or wider, within the bound.
No kernel may reach another device: no remote copies, remote signals or barrier semaphores. Data moves between devices by JAX's collectives and lax.ppermute only.
A program may use at most 64 MiB of HBM per device.

v0:
```python
import jax
import jax.numpy as jnp
from jax import lax
from jax.experimental import pallas as pl
from jax.experimental.pallas import tpu as pltpu
from jax.sharding import PartitionSpec as P


KVH = 8
HD = 128
BLK = 64
NV = 5
NS = 8
NBD = 32
NSLOT = 10
LOG2E = 1.4426950408889634


SCALE = (HD**-0.5) * LOG2E
WROWS = 3 * 2048
G = 4
CH = 2


def attn_kernel(
    tab, q_in, own, swp, pas, sh2, vkv, o_ref, q_ref, ks, vs, bias, s0, s1, m0, m1, p0, p1, l0, l1, sem, sem1
):
    run = tab[0]
    odd = (run & 1) == 1
    copies = [pltpu.make_async_copy(q_in, q_ref, sem.at[0])]
    for n, part in enumerate((ks, vs)):
        for m, src in ((0, sh2), (2, own)):
            copies.append(
                pltpu.make_async_copy(src.at[:, n], part.at[pl.ds(m * 16, 16)], sem.at[1 + 2 * n + m // 2])
            )
        copies.append(pltpu.make_async_copy(vkv.at[n], part.at[pl.ds(48, 5)], sem.at[5 + n]))
    for c in copies:
        c.start()
    for cond, src in ((odd, swp), (jnp.logical_not(odd), pas)):

        @pl.when(cond)
        def _():
            both = [
                pltpu.make_async_copy(src.at[:, n], part.at[pl.ds(16, 16)], sem1.at[n])
                for n, part in enumerate((ks, vs))
            ]
            for c in both:
                c.start()
            for c in both:
                c.wait()

    lane = lax.broadcasted_iota(jnp.int32, (8, 128), 1)
    slash = [[tab[11 + hh * NS + n] for n in range(NS)] for hh in range(2)]
    vert = [[tab[1 + hh * NV + n] for n in range(NV)] for hh in range(2)]
    spans = []
    for hh in range(2):
        named = [0] + slash[hh] + vert[hh]
        spans.append([jnp.where(lane < BLK, named[2 * c], named[2 * c + 1]) for c in range(7)])

    def mask(il, carry):
        for hh in range(2):
            for c in range(7):
                gap = run * NBD + il - spans[hh][c]
                bad = gap < 0
                if c >= 4:
                    hit = gap == 0
                    for s in slash[hh]:
                        hit = hit | (gap == s)
                    if c == 4:
                        hit = hit & (lane >= BLK)
                    bad = bad | hit
                bias[2 * il + hh, :, c * 128 : (c + 1) * 128] = jnp.where(bad, -jnp.inf, 0.0)
        return carry

    lax.fori_loop(0, NBD, mask, 0, unroll=4)
    for c in copies:
        c.wait()

    rr = lax.broadcasted_iota(jnp.int32, (BLK, 128), 0)
    cc = lax.broadcasted_iota(jnp.int32, (BLK, 128), 1)
    causal = (rr >= cc) | (cc >= BLK)
    scores = (s0, s1)
    maxima = (m0, m1)
    probs = (p0, p1)
    totals = (l0, l1)
    ksv = ks.reshape(53 * 128, HD)
    vsv = vs.reshape(53 * 128, HD)

    def rows_of(part, hh, il, n):
        if n <= NS:
            at = (2 * NBD + il) * BLK
            if n > 0:
                at = at - slash[hh][n - 1] * BLK
            return part[pl.ds(pl.multiple_of(at, BLK), BLK), :]
        at = WROWS + (hh * NV + n - NS - 1) * BLK
        return part[at : at + BLK, :]

    def first(t, buf):
        for g in range(G):
            il = t * (G // 2) + g // 2
            hh = g % 2
            row = pl.multiple_of(il * BLK, BLK)
            q = q_ref[pl.ds(row, BLK), hh * HD : (hh + 1) * HD]
            m = None
            for c0 in range(0, 7, CH):
                cs = list(range(c0, min(7, c0 + CH)))
                k = jnp.concatenate([rows_of(ksv, hh, il, 2 * c + j) for c in cs for j in range(2)], axis=0)
                xx = lax.dot_general(q, k, (((1,), (1,)), ((), ())), preferred_element_type=jnp.float32)
                for c in cs:
                    x = xx[:, (c - c0) * 128 : (c - c0 + 1) * 128]
                    x = x.reshape(8, 8, 128) + bias[2 * il + hh, :, c * 128 : (c + 1) * 128][None]
                    x = x.reshape(BLK, 128)
                    if c == 0:
                        x = jnp.where(causal, x, -jnp.inf)
                    scores[buf][g, :, c * 128 : (c + 1) * 128] = x
                    m = x if m is None else jnp.maximum(m, x)
            m = jnp.max(m, axis=1, keepdims=True)
            maxima[buf][g] = jnp.broadcast_to(m, (BLK, 128))

    def second(t, buf):
        for g in range(G):
            m = maxima[buf][g]
            total = None
            for c in range(7):
                p = jnp.exp2((scores[buf][g, :, c * 128 : (c + 1) * 128] - m) * SCALE)
                total = p if total is None else total + p
                probs[buf][g, :, c * 128 : (c + 1) * 128] = p.astype(jnp.bfloat16)
            total = jnp.sum(total, axis=1, keepdims=True)
            totals[buf][g] = jnp.broadcast_to(1.0 / total, (BLK, 128))

    def third(t, buf):
        for g in range(G):
            il = t * (G // 2) + g // 2
            hh = g % 2
            row = pl.multiple_of(il * BLK, BLK)
            v = jnp.concatenate([rows_of(vsv, hh, il, n) for n in range(14)], axis=0)
            acc = jnp.dot(probs[buf][g], v, preferred_element_type=jnp.float32)
            o_ref[pl.ds(row, BLK), hh * HD : (hh + 1) * HD] = (acc * totals[buf][g]).astype(o_ref.dtype)

    steps = 2 * NBD // G
    first(0, 0)
    first(1, 1)
    second(0, 0)

    def body(u, carry):
        t = 2 * u
        for e in range(2):
            third(t + e, e)
            first(jnp.minimum(t + e + 2, steps - 1), e)
            second(jnp.minimum(t + e + 1, steps - 1), 1 - e)
        return carry

    lax.fori_loop(0, steps // 2, body, 0)


def attend(tab, q, own, swp, pas, sh2, vkv):
    hbm = pl.BlockSpec(memory_space=pl.ANY)
    smem = pl.BlockSpec(memory_space=pltpu.SMEM)
    vmem = pl.BlockSpec(memory_space=pltpu.VMEM)
    return pl.pallas_call(
        attn_kernel,
        out_shape=jax.ShapeDtypeStruct((NBD * BLK, 2 * HD), jnp.bfloat16),
        in_specs=[smem] + [hbm] * 6,
        out_specs=vmem,
        scratch_shapes=[
            pltpu.VMEM((NBD * BLK, 2 * HD), jnp.bfloat16),
            pltpu.VMEM((53, 128, HD), jnp.bfloat16),
            pltpu.VMEM((53, 128, HD), jnp.bfloat16),
            pltpu.VMEM((2 * NBD, 8, 896), jnp.float32),
            pltpu.VMEM((G, BLK, 896), jnp.float32),
            pltpu.VMEM((G, BLK, 896), jnp.float32),
            pltpu.VMEM((G, BLK, 128), jnp.float32),
            pltpu.VMEM((G, BLK, 128), jnp.float32),
            pltpu.VMEM((G, BLK, 896), jnp.bfloat16),
            pltpu.VMEM((G, BLK, 896), jnp.bfloat16),
            pltpu.VMEM((G, BLK, 128), jnp.float32),
            pltpu.VMEM((G, BLK, 128), jnp.float32),
            pltpu.SemaphoreType.DMA((7,)),
            pltpu.SemaphoreType.DMA((2,)),
        ],
        cost_estimate=pl.CostEstimate(flops=2_000_000_000, bytes_accessed=6_000_000, transcendentals=4_000_000),
        name="attend",
    )(tab, q, own, swp, pas, sh2, vkv)


def pick_kernel(tab, kv, o_ref, buf, sem):
    run = tab[0]
    picked = []
    copies = []
    for n in range(NSLOT):
        local = tab[1 + n] - run * NBD
        at = jnp.clip(local, 0, NBD - 1)
        picked.append(local == at)
        rows = pl.ds(pl.multiple_of((at & 1) * BLK, BLK), BLK)
        for part in range(2):
            copies.append(pltpu.make_async_copy(kv.at[at >> 1, part, rows], buf.at[n, part], sem.at[n, part]))
    for c in copies:
        c.start()
    for c in copies:
        c.wait()
    for n in range(NSLOT):
        ok = jnp.full((BLK, HD), jnp.where(picked[n], 1, 0), jnp.int32) == 1
        for part in range(2):
            x = buf[n, part].astype(jnp.float32)
            dst = (part * NSLOT + n) * BLK
            o_ref[dst : dst + BLK, :] = jnp.where(ok, x, 0.0).astype(jnp.bfloat16)


def pick(tab, kv):
    return pl.pallas_call(
        pick_kernel,
        out_shape=jax.ShapeDtypeStruct((NSLOT * 128, HD), jnp.bfloat16),
        in_specs=[pl.BlockSpec(memory_space=pltpu.SMEM), pl.BlockSpec(memory_space=pl.ANY)],
        out_specs=pl.BlockSpec(memory_space=pltpu.VMEM),
        scratch_shapes=[
            pltpu.VMEM((NSLOT, 2, BLK, HD), jnp.bfloat16),
            pltpu.SemaphoreType.DMA((NSLOT, 2)),
        ],
        cost_estimate=pl.CostEstimate(flops=1_000_000, bytes_accessed=1_500_000, transcendentals=0),
        name="pick",
    )(tab, kv)


def by_head(k, v):
    rows = k.shape[0]
    k3 = k.reshape(rows, KVH, HD).transpose(1, 0, 2)
    v3 = v.reshape(rows, KVH, HD).transpose(1, 0, 2)
    return jnp.repeat(jnp.stack([k3, v3], axis=1), 2, axis=0)


def exchange(x, axis):
    return lax.all_to_all(x, axis, split_axis=0, concat_axis=0, tiled=True)


def per_device(queries, key_states, value_states, vertical_blocks, slash_offsets):
    runs = lax.axis_size("qblk")
    head = lax.axis_index("head")
    run = lax.axis_index("qblk").astype(jnp.int32)
    ahead = [(r, (r + 2) % runs) for r in range(runs)]
    swap = [(r, r ^ 1) for r in range(runs)]
    mine = lambda t: lax.dynamic_slice_in_dim(t, 2 * head, 2, 0).reshape(-1)
    tab = jnp.concatenate([run.reshape(1), mine(vertical_blocks), mine(slash_offsets)])
    own = exchange(by_head(key_states, value_states), "head")
    own, tab = lax.optimization_barrier((own, tab))
    cand = pick(tab, own).reshape(runs, NSLOT * 128 // runs, HD)
    cand = exchange(cand, "qblk")
    sh2 = lax.ppermute(own, "qblk", ahead)
    swp = lax.ppermute(own, "qblk", swap)
    pas = lax.ppermute(sh2, "qblk", swap)
    part = jnp.sum(cand.astype(jnp.float32), axis=0).astype(jnp.bfloat16)
    vert = lax.all_gather(part, "qblk", axis=0, tiled=True)
    q = lax.all_to_all(queries, "head", split_axis=1, concat_axis=0, tiled=True)
    out = attend(tab, q, own, swp, pas, sh2, vert.reshape(2, NSLOT // 2, 128, HD))
    return lax.all_to_all(out, "head", split_axis=0, concat_axis=1, tiled=True)


def solution(mesh):
    spec = P(("qblk", "head"), None)
    return jax.shard_map(
        per_device,
        mesh=mesh,
        in_specs=(spec, spec, spec, P(), P()),
        out_specs=spec,
        check_vma=False,
    )
```

profile of v0, /device:TPU:1, one launch (start us, length us, event | category | flops | bytes accessed | tf_op | source)
XLA Modules:
  0.0 125.4 jit_solution(7829812626022822688)
XLA Ops:
  0.0 1.0 copy.13
  1.2 0.1 copy.6
  1.3 1.2 broadcast_in_dim.3
  2.5 7.7 %all-to-all-start = ((bf16[16,2,128,128]{3,2,1,0:T(8,128)(2,1)}), bf16[16,2,128,128]{3,2,1,0:T(8,128)(2,1)S(1)}, u32[]{:S(2)}, u32[]{:S(2)}) async-start(bf16[16,2,128,128]{3,2,1,0:T(8,128)(2,1)} %bitcast.4), calls=%async_computation | async-start | bytes 2097152 | tf_op jit(solution)/shard_map/all_to_all | solution.py:232
  10.3 0.1 copy.7
  10.4 0.1 reshape.34
  10.6 0.1 copy.8
  10.6 0.1 reshape.35
  10.7 0.6 pad_add_fusion.tab
  11.4 14.5 %all-to-all-done.kv.own = bf16[16,2,128,128]{3,2,1,0:T(8,128)(2,1)S(1)} async-done(((bf16[16,2,128,128]{3,2,1,0:T(8,128)(2,1)}), bf16[16,2,128,128]{3,2,1,0:T(8,128)(2,1)S(1)}, u32[]{:S(2)}, u32[]{:S(2)}) %all-to-all-start) | async-done | bytes 1048608 | tf_op jit(solution)/shard_map/all_to_all | solution.py:232
  25.9 1.6 %collective-permute-start.1 = (bf16[16,2,128,128]{3,2,1,0:T(8,128)(2,1)S(1)}, bf16[16,2,128,128]{3,2,1,0:T(8,128)(2,1)S(1)}, u32[]{:S(2)}, u32[]{:S(2)}) collective-permute-start(bf16[16,2,128,128]{3,2,1,0:T(8,128)(2,1)S(1)} %all-to-all-done.kv.own), channel_id=1, source_target_pairs={{0,2},{1,3},{2,4},{3,5},{4,6},{5,7},{6,8},{7,9},{8,10},{9,11},{10,... | collective-permute-start | bytes 3145736 | tf_op jit(solution)/shard_map/ppermute | solution.py:247
  27.5 2.7 %pick.1 = bf16[1280,128]{1,0:T(8,128)(2,1)} custom-call(s32[27]{0:T(128)} %pad_add_fusion.tab, bf16[16,2,128,128]{3,2,1,0:T(8,128)(2,1)} %copy-done.1), custom_call_target="tpu_custom_call" | custom-call | flops 1000000 | bytes 1500000 | tf_op jit(solution)/shard_map/pick/pallas_call | solution.py:210
  30.2 10.9 %all-to-all-start.2 = ((bf16[16,80,128]{2,1,0:T(8,128)(2,1)}), bf16[16,80,128]{2,1,0:T(8,128)(2,1)S(1)}, u32[]{:S(2)}, u32[]{:S(2)}) async-start(bf16[16,80,128]{2,1,0:T(8,128)(2,1)} %bitcast.28), calls=%async_computation.2 | async-start | bytes 655360 | tf_op jit(solution)/shard_map/all_to_all | solution.py:232
  41.2 0.2 collective-permute-start
  41.3 10.6 %collective-permute-done.1.sh2 = bf16[16,2,128,128]{3,2,1,0:T(8,128)(2,1)S(1)} collective-permute-done((bf16[16,2,128,128]{3,2,1,0:T(8,128)(2,1)S(1)}, bf16[16,2,128,128]{3,2,1,0:T(8,128)(2,1)S(1)}, u32[]{:S(2)}, u32[]{:S(2)}) %collective-permute-start.1) | collective-permute-done | bytes 1048608 | tf_op jit(solution)/shard_map/ppermute | solution.py:247
  51.9 7.1 %collective-permute-start.2 = (bf16[16,2,128,128]{3,2,1,0:T(8,128)(2,1)S(1)}, bf16[16,2,128,128]{3,2,1,0:T(8,128)(2,1)}, u32[]{:S(2)}, u32[]{:S(2)}) collective-permute-start(bf16[16,2,128,128]{3,2,1,0:T(8,128)(2,1)S(1)} %collective-permute-done.1.sh2), channel_id=1, source_target_pairs={{0,1},{1,0},{2,3},{3,2},{4,5},{5,4},{6,7},{7,6},{8,9},{9,8},{10,11... | collective-permute-start | bytes 3145736 | tf_op jit(solution)/shard_map/ppermute | solution.py:249
  59.1 1.1 copy.16
  60.1 2.3 %all-to-all-done.2 = bf16[16,80,128]{2,1,0:T(8,128)(2,1)S(1)} async-done(((bf16[16,80,128]{2,1,0:T(8,128)(2,1)}), bf16[16,80,128]{2,1,0:T(8,128)(2,1)S(1)}, u32[]{:S(2)}, u32[]{:S(2)}) %all-to-all-start.2) | async-done | bytes 327712 | tf_op jit(solution)/shard_map/all_to_all | solution.py:232
  62.4 3.9 %all-to-all-start.1 = ((bf16[128,16,256]{2,0,1:T(8,128)(2,1)}), bf16[128,16,256]{2,0,1:T(8,128)(2,1)S(1)}, u32[]{:S(2)}, u32[]{:S(2)}) async-start(bf16[128,16,256]{2,0,1:T(8,128)(2,1)} %bitcast.26), calls=%async_computation.1 | async-start | bytes 2097152 | tf_op jit(solution)/shard_map/all_to_all | solution.py:252
  66.4 18.4 %all_gather.3 = bf16[1280,128]{1,0:T(8,128)(2,1)} all-gather(bf16[80,128]{1,0:T(8,128)(2,1)S(1)} %reduce_sum.12), channel_id=1, replica_groups=mesh['head'=16,'qblk'=16] {'qblk'}, dimensions={0}, use_global_device_ids=true | all-gather | bytes 348160 | tf_op jit(solution)/shard_map/all_gather | solution.py:251
  84.8 1.0 copy-done.3
  85.8 15.8 %attend.1 = bf16[2048,256]{1,0:T(8,128)(2,1)} custom-call(s32[27]{0:T(128)} %pad_add_fusion.tab, bf16[2048,256]{1,0:T(8,128)(2,1)} %bitcast.30, bf16[16,2,128,128]{3,2,1,0:T(8,128)(2,1)} %copy-done.1, bf16[16,2,128,128]{3,2,1,0:T(8,128)(2,1)} %collective-permute-done.swp, bf16[16,2,128,128]{3,2,1,0:T(8,128)(2,1)} %collective-permute-done.2.pas, ...), custom_call_target="tpu_custom_call" | custom-call | flops 2000000000 | bytes 6000000 | tf_op jit(solution)/shard_map/attend/pallas_call | solution.py:160
  101.5 22.7 %all_to_all.48 = bf16[16,128,256]{2,1,0:T(8,128)(2,1)S(1)} all-to-all(bf16[16,128,256]{2,1,0:T(8,128)(2,1)} %bitcast.31), channel_id=1, replica_groups=mesh['head'=16,'qblk'=16] {'head'}, dimensions={0} | all-to-all | bytes 2097152 | tf_op jit(solution)/shard_map/all_to_all | solution.py:254
  124.3 1.1 copy.12
  (21 shorter events, 0.3 us)
Async XLA Ops:
  0.0 10.5 %copy-start = (s32[32,8]{0,1:T(8,128)S(1)}, s32[32,8]{0,1:T(8,128)}, u32[]{:S(2)}) copy-start(s32[32,8]{0,1:T(8,128)} %param.9) | copy-start | bytes 3076
  0.0 1.0 copy-start.4
  2.5 7.7 %copy-start.5 = (s32[32,5]{0,1:T(8,128)S(1)}, s32[32,5]{0,1:T(8,128)}, u32[]{:S(2)}) copy-start(s32[32,5]{0,1:T(8,128)} %param.8) | copy-start | bytes 1924
  2.5 23.4 %all-to-all-start = ((bf16[16,2,128,128]{3,2,1,0:T(8,128)(2,1)}), bf16[16,2,128,128]{3,2,1,0:T(8,128)(2,1)S(1)}, u32[]{:S(2)}, u32[]{:S(2)}) async-start(bf16[16,2,128,128]{3,2,1,0:T(8,128)(2,1)} %bitcast.4), calls=%async_computation | async-start | bytes 2097152 | tf_op jit(solution)/shard_map/all_to_all | solution.py:232
  10.2 48.9 %copy-start.2 = (bf16[128,4096]{1,0:T(8,128)(2,1)S(1)}, bf16[128,4096]{1,0:T(8,128)(2,1)}, u32[]{:S(2)}) copy-start(bf16[128,4096]{1,0:T(8,128)(2,1)} %param.5) | copy-start | bytes 3145732
  25.9 1.6 %copy-start.1 = (bf16[16,2,128,128]{3,2,1,0:T(8,128)(2,1)}, bf16[16,2,128,128]{3,2,1,0:T(8,128)(2,1)S(1)}, u32[]{:S(2)}) copy-start(bf16[16,2,128,128]{3,2,1,0:T(8,128)(2,1)S(1)} %all-to-all-done.kv.own) | copy-start | bytes 3145732
  25.9 26.1 %collective-permute-start.1 = (bf16[16,2,128,128]{3,2,1,0:T(8,128)(2,1)S(1)}, bf16[16,2,128,128]{3,2,1,0:T(8,128)(2,1)S(1)}, u32[]{:S(2)}, u32[]{:S(2)}) collective-permute-start(bf16[16,2,128,128]{3,2,1,0:T(8,128)(2,1)S(1)} %all-to-all-done.kv.own), channel_id=1, source_target_pairs={{0,2},{1,3},{2,4},{3,5},{4,6},{5,7},{6,8},{7,9},{8,10},{9,11},{10,... | collective-permute-start | bytes 3145736 | tf_op jit(solution)/shard_map/ppermute | solution.py:247
  30.2 32.2 %all-to-all-start.2 = ((bf16[16,80,128]{2,1,0:T(8,128)(2,1)}), bf16[16,80,128]{2,1,0:T(8,128)(2,1)S(1)}, u32[]{:S(2)}, u32[]{:S(2)}) async-start(bf16[16,80,128]{2,1,0:T(8,128)(2,1)} %bitcast.28), calls=%async_computation.2 | async-start | bytes 655360 | tf_op jit(solution)/shard_map/all_to_all | solution.py:232
  41.2 43.6 %collective-permute-start = (bf16[16,2,128,128]{3,2,1,0:T(8,128)(2,1)}, bf16[16,2,128,128]{3,2,1,0:T(8,128)(2,1)}, u32[]{:S(2)}, u32[]{:S(2)}) collective-permute-start(bf16[16,2,128,128]{3,2,1,0:T(8,128)(2,1)} %copy-done.1), channel_id=1, source_target_pairs={{0,1},{1,0},{2,3},{3,2},{4,5},{5,4},{6,7},{7,6},{8,9},{9,8},{10,11... | collective-permute-start | bytes 3145736 | tf_op jit(solution)/shard_map/ppermute | solution.py:248
  51.9 8.2 %copy-start.6 = (bf16[16,2,128,128]{3,2,1,0:T(8,128)(2,1)}, bf16[16,2,128,128]{3,2,1,0:T(8,128)(2,1)S(1)}, u32[]{:S(2)}) copy-start(bf16[16,2,128,128]{3,2,1,0:T(8,128)(2,1)S(1)} %collective-permute-done.1.sh2) | copy-start | bytes 3145732
  51.9 32.9 %collective-permute-start.2 = (bf16[16,2,128,128]{3,2,1,0:T(8,128)(2,1)S(1)}, bf16[16,2,128,128]{3,2,1,0:T(8,128)(2,1)}, u32[]{:S(2)}, u32[]{:S(2)}) collective-permute-start(bf16[16,2,128,128]{3,2,1,0:T(8,128)(2,1)S(1)} %collective-permute-done.1.sh2), channel_id=1, source_target_pairs={{0,1},{1,0},{2,3},{3,2},{4,5},{5,4},{6,7},{7,6},{8,9},{9,8},{10,11... | collective-permute-start | bytes 3145736 | tf_op jit(solution)/shard_map/ppermute | solution.py:249
  62.4 22.4 %all-to-all-start.1 = ((bf16[128,16,256]{2,0,1:T(8,128)(2,1)}), bf16[128,16,256]{2,0,1:T(8,128)(2,1)S(1)}, u32[]{:S(2)}, u32[]{:S(2)}) async-start(bf16[128,16,256]{2,0,1:T(8,128)(2,1)} %bitcast.26), calls=%async_computation.1 | async-start | bytes 2097152 | tf_op jit(solution)/shard_map/all_to_all | solution.py:252
  84.8 1.0 copy-start.3
where the time goes:
time: 126 us; the launch traced here: 125 us
  blocking collectives  41.2 us (33%)
  starting transfers between devices  31.5 us (25%)
  waiting for transfers between devices  27.4 us (22%)
  Pallas kernels  18.5 us (15%)
  local copies, waits for them, and re-layouts  6.01 us (5%)
    all_to_all x1, blocking collectives, per_device(): return lax.all_to_all(out, 'head', split_axis=0, concat_axis=1, tiled=True)  22.7 us
    all_to_all x2, starting transfers between devices, exchange(): return lax.all_to_all(x, axis, split_axis=0, concat_axis=0, tiled=True)  18.6 us
    all_gather x1, blocking collectives, per_device(): vert = lax.all_gather(part, 'qblk', axis=0, tiled=True)  18.4 us
    all_to_all x2, waiting for transfers between devices, exchange(): return lax.all_to_all(x, axis, split_axis=0, concat_axis=0, tiled=True)  16.8 us
    pallas_call x1, Pallas kernels, attend(): pl.pallas_call(attn_kernel, out_shape=jax.ShapeDtypeStruct((NBD * BLK, 2...  15.8 us
    ppermute x1, waiting for transfers between devices, per_device(): sh2 = lax.ppermute(own, 'qblk', ahead)  10.6 us
    ppermute x1, starting transfers between devices, per_device(): pas = lax.ppermute(sh2, 'qblk', swap)  7.13 us
    all_to_all x1, starting transfers between devices, per_device(): q = lax.all_to_all(queries, 'head', split_axis=1, concat_axis=0, tiled=True)  3.89 us
  transfers between devices with their start and end apart: 6, of which 3 were waited for; matrix products, arithmetic and copies ran while one was open for 2% of the time, Pallas kernels for 2%

commit v1 on v0

--- a/solution.py
+++ b/solution.py
@@ -12,7 +12,7 @@
 NV = 5
 NS = 8
 NBD = 32
-NSLOT = 10
+NSLOT = 8
 LOG2E = 1.4426950408889634
 
 
@@ -33,7 +33,7 @@
             copies.append(
                 pltpu.make_async_copy(src.at[:, n], part.at[pl.ds(m * 16, 16)], sem.at[1 + 2 * n + m // 2])
             )
-        copies.append(pltpu.make_async_copy(vkv.at[n], part.at[pl.ds(48, 5)], sem.at[5 + n]))
+        copies.append(pltpu.make_async_copy(vkv.at[n], part.at[pl.ds(48, NSLOT // 2)], sem.at[5 + n]))
     for c in copies:
         c.start()
     for cond, src in ((odd, swp), (jnp.logical_not(odd), pas)):
@@ -50,8 +50,8 @@
                 c.wait()
 
     lane = lax.broadcasted_iota(jnp.int32, (8, 128), 1)
-    slash = [[tab[11 + hh * NS + n] for n in range(NS)] for hh in range(2)]
-    vert = [[tab[1 + hh * NV + n] for n in range(NV)] for hh in range(2)]
+    slash = [[tab[19 + hh * NS + n] for n in range(NS)] for hh in range(2)]
+    vert = [[tab[9 + hh * NV + n] for n in range(NV)] for hh in range(2)]
     spans = []
     for hh in range(2):
         named = [0] + slash[hh] + vert[hh]
@@ -83,8 +83,8 @@
     maxima = (m0, m1)
     probs = (p0, p1)
     totals = (l0, l1)
-    ksv = ks.reshape(53 * 128, HD)
-    vsv = vs.reshape(53 * 128, HD)
+    ksv = ks.reshape(52 * 128, HD)
+    vsv = vs.reshape(52 * 128, HD)
 
     def rows_of(part, hh, il, n):
         if n <= NS:
@@ -92,8 +92,8 @@
             if n > 0:
                 at = at - slash[hh][n - 1] * BLK
             return part[pl.ds(pl.multiple_of(at, BLK), BLK), :]
-        at = WROWS + (hh * NV + n - NS - 1) * BLK
-        return part[at : at + BLK, :]
+        slot = n - NS - 1 if hh == 0 else tab[35 + n - NS - 1]
+        return part[pl.ds(pl.multiple_of(WROWS + slot * BLK, BLK), BLK), :]
 
     def first(t, buf):
         for g in range(G):
@@ -164,8 +164,8 @@
         out_specs=vmem,
         scratch_shapes=[
             pltpu.VMEM((NBD * BLK, 2 * HD), jnp.bfloat16),
-            pltpu.VMEM((53, 128, HD), jnp.bfloat16),
-            pltpu.VMEM((53, 128, HD), jnp.bfloat16),
+            pltpu.VMEM((52, 128, HD), jnp.bfloat16),
+            pltpu.VMEM((52, 128, HD), jnp.bfloat16),
             pltpu.VMEM((2 * NBD, 8, 896), jnp.float32),
             pltpu.VMEM((G, BLK, 896), jnp.float32),
             pltpu.VMEM((G, BLK, 896), jnp.float32),
@@ -183,42 +183,43 @@
     )(tab, q, own, swp, pas, sh2, vkv)
 
 
-def pick_kernel(tab, kv, o_ref, buf, sem):
+def pick_kernel(tab, kv, o_ref):
     run = tab[0]
-    picked = []
-    copies = []
     for n in range(NSLOT):
         local = tab[1 + n] - run * NBD
         at = jnp.clip(local, 0, NBD - 1)
-        picked.append(local == at)
         rows = pl.ds(pl.multiple_of((at & 1) * BLK, BLK), BLK)
+        ok = jnp.full((BLK, HD), jnp.where(local == at, 1, 0), jnp.int32) == 1
         for part in range(2):
-            copies.append(pltpu.make_async_copy(kv.at[at >> 1, part, rows], buf.at[n, part], sem.at[n, part]))
-    for c in copies:
-        c.start()
-    for c in copies:
-        c.wait()
-    for n in range(NSLOT):
-        ok = jnp.full((BLK, HD), jnp.where(picked[n], 1, 0), jnp.int32) == 1
-        for part in range(2):
-            x = buf[n, part].astype(jnp.float32)
+            x = kv[at >> 1, part, rows].astype(jnp.float32)
             dst = (part * NSLOT + n) * BLK
             o_ref[dst : dst + BLK, :] = jnp.where(ok, x, 0.0).astype(jnp.bfloat16)
 
 
 def pick(tab, kv):
+    vmem = pl.BlockSpec(memory_space=pltpu.VMEM)
     return pl.pallas_call(
         pick_kernel,
         out_shape=jax.ShapeDtypeStruct((NSLOT * 128, HD), jnp.bfloat16),
-        in_specs=[pl.BlockSpec(memory_space=pltpu.SMEM), pl.BlockSpec(memory_space=pl.ANY)],
-        out_specs=pl.BlockSpec(memory_space=pltpu.VMEM),
-        scratch_shapes=[
-            pltpu.VMEM((NSLOT, 2, BLK, HD), jnp.bfloat16),
-            pltpu.SemaphoreType.DMA((NSLOT, 2)),
-        ],
+        in_specs=[pl.BlockSpec(memory_space=pltpu.SMEM), vmem],
+        out_specs=vmem,
         cost_estimate=pl.CostEstimate(flops=1_000_000, bytes_accessed=1_500_000, transcendentals=0),
         name="pick",
     )(tab, kv)
+
+
+def table(vertical_blocks, slash_offsets, head, run):
+    vert = lax.dynamic_slice_in_dim(vertical_blocks, 2 * head, 2, 0)
+    slash = lax.dynamic_slice_in_dim(slash_offsets, 2 * head, 2, 0)
+    same = vert[1][:, None] == vert[0][None, :]
+    fresh = jnp.logical_not(jnp.any(same, axis=1))
+    n = jnp.arange(NV, dtype=jnp.int32)
+    rank = jnp.sum(jnp.where((n[None, :] < n[:, None]) & fresh[None, :], 1, 0), axis=1)
+    slot = jnp.where(fresh, NV + rank, jnp.sum(jnp.where(same, n[None, :], 0), axis=1))
+    chosen = fresh[None, :] & (rank[None, :] == n[: NSLOT - NV, None])
+    extra = jnp.sum(jnp.where(chosen, vert[1][None, :], 0), axis=1)
+    parts = [run.reshape(1), vert[0], extra, vert.reshape(-1), slash.reshape(-1), slot]
+    return jnp.concatenate([p.astype(jnp.int32) for p in parts])
 
 
 def by_head(k, v):
@@ -238,8 +239,7 @@
     run = lax.axis_index("qblk").astype(jnp.int32)
     ahead = [(r, (r + 2) % runs) for r in range(runs)]
     swap = [(r, r ^ 1) for r in range(runs)]
-    mine = lambda t: lax.dynamic_slice_in_dim(t, 2 * head, 2, 0).reshape(-1)
-    tab = jnp.concatenate([run.reshape(1), mine(vertical_blocks), mine(slash_offsets)])
+    tab = table(vertical_blocks, slash_offsets, head, run)
     own = exchange(by_head(key_states, value_states), "head")
     own, tab = lax.optimization_barrier((own, tab))
     cand = pick(tab, own).reshape(runs, NSLOT * 128 // runs, HD)

time: 126 us -> 125 us (level)
  no operation moved by 1% of the time
where the time goes in v1:
time: 125 us; the launch traced here: 124 us
  blocking collectives  40.8 us (33%)
  starting transfers between devices  30.7 us (25%)
  waiting for transfers between devices  27 us (22%)
  Pallas kernels  18.1 us (14%)
  local copies, waits for them, and re-layouts  6.77 us (5%)
    all_to_all x1, blocking collectives, per_device(): return lax.all_to_all(out, 'head', split_axis=0, concat_axis=1, tiled=True)  22.7 us
    all_to_all x2, starting transfers between devices, exchange(): return lax.all_to_all(x, axis, split_axis=0, concat_axis=0, tiled=True)  18.6 us
    all_gather x1, blocking collectives, per_device(): vert = lax.all_gather(part, 'qblk', axis=0, tiled=True)  18 us
    pallas_call x1, Pallas kernels, attend(): pl.pallas_call(attn_kernel, out_shape=jax.ShapeDtypeStruct((NBD * BLK, 2...  16.1 us
    all_to_all x2, waiting for transfers between devices, exchange(): return lax.all_to_all(x, axis, split_axis=0, concat_axis=0, tiled=True)  15.6 us
    ppermute x1, waiting for transfers between devices, per_device(): sh2 = lax.ppermute(own, 'qblk', ahead)  11.4 us
    ppermute x1, starting transfers between devices, per_device(): pas = lax.ppermute(sh2, 'qblk', swap)  6.42 us
    all_to_all x1, starting transfers between devices, per_device(): q = lax.all_to_all(queries, 'head', split_axis=1, concat_axis=0, tiled=True)  3.89 us
  transfers between devices with their start and end apart: 6, of which 3 were waited for; matrix products, arithmetic and copies ran while one was open for 2% of the time, Pallas kernels for 2%

profile of v1, /device:TPU:1, one launch (start us, length us, event | category | flops | bytes accessed | tf_op | source)
XLA Modules:
  0.0 124.2 jit_solution(14739110864886860226)
XLA Ops:
  0.0 1.0 copy.18
  1.3 1.2 broadcast_in_dim.38
  2.5 7.7 %all-to-all-start = ((bf16[16,2,128,128]{3,2,1,0:T(8,128)(2,1)}), bf16[16,2,128,128]{3,2,1,0:T(8,128)(2,1)S(1)}, u32[]{:S(2)}, u32[]{:S(2)}) async-start(bf16[16,2,128,128]{3,2,1,0:T(8,128)(2,1)} %bitcast.4), calls=%async_computation | async-start | bytes 2097152 | tf_op jit(solution)/shard_map/all_to_all | solution.py:233
  10.3 0.1 copy.12
  10.5 0.2 slice_reduce_fusion
  10.7 0.2 compare_reduce_fusion
  11.1 0.2 fusion
  11.3 0.2 select_reduce_fusion.1
  11.5 0.6 concatenate.3.tab
  12.1 13.8 %all-to-all-done.kv.own = bf16[16,2,128,128]{3,2,1,0:T(8,128)(2,1)S(1)} async-done(((bf16[16,2,128,128]{3,2,1,0:T(8,128)(2,1)}), bf16[16,2,128,128]{3,2,1,0:T(8,128)(2,1)S(1)}, u32[]{:S(2)}, u32[]{:S(2)}) %all-to-all-start) | async-done | bytes 1048608 | tf_op jit(solution)/shard_map/all_to_all | solution.py:233
  25.9 1.6 %collective-permute-start.1 = (bf16[16,2,128,128]{3,2,1,0:T(8,128)(2,1)S(1)}, bf16[16,2,128,128]{3,2,1,0:T(8,128)(2,1)S(1)}, u32[]{:S(2)}, u32[]{:S(2)}) collective-permute-start(bf16[16,2,128,128]{3,2,1,0:T(8,128)(2,1)S(1)} %all-to-all-done.kv.own), channel_id=1, source_target_pairs={{0,2},{1,3},{2,4},{3,5},{4,6},{5,7},{6,8},{7,9},{8,10},{9,11},{10,... | collective-permute-start | bytes 3145736 | tf_op jit(solution)/shard_map/ppermute | solution.py:247
  27.5 2.0 %pick.1 = bf16[1024,128]{1,0:T(8,128)(2,1)} custom-call(s32[40]{0:T(128)} %concatenate.3.tab, bf16[16,2,128,128]{3,2,1,0:T(8,128)(2,1)} %copy-done.1), custom_call_target="tpu_custom_call" | custom-call | flops 1000000 | bytes 1500000 | tf_op jit(solution)/shard_map/pick/pallas_call | solution.py:201
  29.5 10.9 %all-to-all-start.2 = ((bf16[16,64,128]{2,1,0:T(8,128)(2,1)}), bf16[16,64,128]{2,1,0:T(8,128)(2,1)S(1)}, u32[]{:S(2)}, u32[]{:S(2)}) async-start(bf16[16,64,128]{2,1,0:T(8,128)(2,1)} %bitcast.29), calls=%async_computation.2 | async-start | bytes 524288 | tf_op jit(solution)/shard_map/all_to_all | solution.py:233
  40.4 0.2 collective-permute-start
  40.6 11.4 %collective-permute-done.1.sh2 = bf16[16,2,128,128]{3,2,1,0:T(8,128)(2,1)S(1)} collective-permute-done((bf16[16,2,128,128]{3,2,1,0:T(8,128)(2,1)S(1)}, bf16[16,2,128,128]{3,2,1,0:T(8,128)(2,1)S(1)}, u32[]{:S(2)}, u32[]{:S(2)}) %collective-permute-start.1) | collective-permute-done | bytes 1048608 | tf_op jit(solution)/shard_map/ppermute | solution.py:247
  51.9 6.4 %collective-permute-start.2 = (bf16[16,2,128,128]{3,2,1,0:T(8,128)(2,1)S(1)}, bf16[16,2,128,128]{3,2,1,0:T(8,128)(2,1)}, u32[]{:S(2)}, u32[]{:S(2)}) collective-permute-start(bf16[16,2,128,128]{3,2,1,0:T(8,128)(2,1)S(1)} %collective-permute-done.1.sh2), channel_id=1, source_target_pairs={{0,1},{1,0},{2,3},{3,2},{4,5},{5,4},{6,7},{7,6},{8,9},{9,8},{10,11... | collective-permute-start | bytes 3145736 | tf_op jit(solution)/shard_map/ppermute | solution.py:249
  58.4 1.1 copy.21
  59.4 1.8 %all-to-all-done.2 = bf16[16,64,128]{2,1,0:T(8,128)(2,1)S(1)} async-done(((bf16[16,64,128]{2,1,0:T(8,128)(2,1)}), bf16[16,64,128]{2,1,0:T(8,128)(2,1)S(1)}, u32[]{:S(2)}, u32[]{:S(2)}) %all-to-all-start.2) | async-done | bytes 262176 | tf_op jit(solution)/shard_map/all_to_all | solution.py:233
  61.2 3.9 %all-to-all-start.1 = ((bf16[128,16,256]{2,0,1:T(8,128)(2,1)}), bf16[128,16,256]{2,0,1:T(8,128)(2,1)S(1)}, u32[]{:S(2)}, u32[]{:S(2)}) async-start(bf16[128,16,256]{2,0,1:T(8,128)(2,1)} %bitcast.26), calls=%async_computation.1 | async-start | bytes 2097152 | tf_op jit(solution)/shard_map/all_to_all | solution.py:252
  65.2 18.0 %all_gather.3 = bf16[1024,128]{1,0:T(8,128)(2,1)} all-gather(bf16[64,128]{1,0:T(8,128)(2,1)S(1)} %reduce_sum.42), channel_id=1, replica_groups=mesh['head'=16,'qblk'=16] {'qblk'}, dimensions={0}, use_global_device_ids=true | all-gather | bytes 278528 | tf_op jit(solution)/shard_map/all_gather | solution.py:251
  83.2 1.0 copy-done.3
  84.2 16.1 %attend.1 = bf16[2048,256]{1,0:T(8,128)(2,1)} custom-call(s32[40]{0:T(128)} %concatenate.3.tab, bf16[2048,256]{1,0:T(8,128)(2,1)} %bitcast.31, bf16[16,2,128,128]{3,2,1,0:T(8,128)(2,1)} %copy-done.1, bf16[16,2,128,128]{3,2,1,0:T(8,128)(2,1)} %collective-permute-done.swp, bf16[16,2,128,128]{3,2,1,0:T(8,128)(2,1)} %collective-permute-done.2.pas, ...), custom_call_target="tpu_custom_call" | custom-call | flops 2000000000 | bytes 6000000 | tf_op jit(solution)/shard_map/attend/pallas_call | solution.py:160
  100.3 22.7 %all_to_all.48 = bf16[16,128,256]{2,1,0:T(8,128)(2,1)S(1)} all-to-all(bf16[16,128,256]{2,1,0:T(8,128)(2,1)} %bitcast.32), channel_id=1, replica_groups=mesh['head'=16,'qblk'=16] {'head'}, dimensions={0} | all-to-all | bytes 2097152 | tf_op jit(solution)/shard_map/all_to_all | solution.py:254
  123.1 1.1 copy.17
  (28 shorter events, 0.7 us)
Async XLA Ops:
  0.0 10.9 %copy-start = (s32[32,8]{0,1:T(8,128)S(1)}, s32[32,8]{0,1:T(8,128)}, u32[]{:S(2)}) copy-start(s32[32,8]{0,1:T(8,128)} %param.9) | copy-start | bytes 3076
  0.0 1.0 copy-start.4
  2.5 7.7 %copy-start.5 = (s32[32,5]{0,1:T(8,128)S(1)}, s32[32,5]{0,1:T(8,128)}, u32[]{:S(2)}) copy-start(s32[32,5]{0,1:T(8,128)} %param.8) | copy-start | bytes 1924
  2.5 23.4 %all-to-all-start = ((bf16[16,2,128,128]{3,2,1,0:T(8,128)(2,1)}), bf16[16,2,128,128]{3,2,1,0:T(8,128)(2,1)S(1)}, u32[]{:S(2)}, u32[]{:S(2)}) async-start(bf16[16,2,128,128]{3,2,1,0:T(8,128)(2,1)} %bitcast.4), calls=%async_computation | async-start | bytes 2097152 | tf_op jit(solution)/shard_map/all_to_all | solution.py:233
  10.2 48.2 %copy-start.2 = (bf16[128,4096]{1,0:T(8,128)(2,1)S(1)}, bf16[128,4096]{1,0:T(8,128)(2,1)}, u32[]{:S(2)}) copy-start(bf16[128,4096]{1,0:T(8,128)(2,1)} %param.5) | copy-start | bytes 3145732
  25.9 1.6 %copy-start.1 = (bf16[16,2,128,128]{3,2,1,0:T(8,128)(2,1)}, bf16[16,2,128,128]{3,2,1,0:T(8,128)(2,1)S(1)}, u32[]{:S(2)}) copy-start(bf16[16,2,128,128]{3,2,1,0:T(8,128)(2,1)S(1)} %all-to-all-done.kv.own) | copy-start | bytes 3145732
  25.9 26.1 %collective-permute-start.1 = (bf16[16,2,128,128]{3,2,1,0:T(8,128)(2,1)S(1)}, bf16[16,2,128,128]{3,2,1,0:T(8,128)(2,1)S(1)}, u32[]{:S(2)}, u32[]{:S(2)}) collective-permute-start(bf16[16,2,128,128]{3,2,1,0:T(8,128)(2,1)S(1)} %all-to-all-done.kv.own), channel_id=1, source_target_pairs={{0,2},{1,3},{2,4},{3,5},{4,6},{5,7},{6,8},{7,9},{8,10},{9,11},{10,... | collective-permute-start | bytes 3145736 | tf_op jit(solution)/shard_map/ppermute | solution.py:247
  29.5 31.7 %all-to-all-start.2 = ((bf16[16,64,128]{2,1,0:T(8,128)(2,1)}), bf16[16,64,128]{2,1,0:T(8,128)(2,1)S(1)}, u32[]{:S(2)}, u32[]{:S(2)}) async-start(bf16[16,64,128]{2,1,0:T(8,128)(2,1)} %bitcast.29), calls=%async_computation.2 | async-start | bytes 524288 | tf_op jit(solution)/shard_map/all_to_all | solution.py:233
  40.4 42.8 %collective-permute-start = (bf16[16,2,128,128]{3,2,1,0:T(8,128)(2,1)}, bf16[16,2,128,128]{3,2,1,0:T(8,128)(2,1)}, u32[]{:S(2)}, u32[]{:S(2)}) collective-permute-start(bf16[16,2,128,128]{3,2,1,0:T(8,128)(2,1)} %copy-done.1), channel_id=1, source_target_pairs={{0,1},{1,0},{2,3},{3,2},{4,5},{5,4},{6,7},{7,6},{8,9},{9,8},{10,11... | collective-permute-start | bytes 3145736 | tf_op jit(solution)/shard_map/ppermute | solution.py:248
  51.9 7.5 %copy-start.6 = (bf16[16,2,128,128]{3,2,1,0:T(8,128)(2,1)}, bf16[16,2,128,128]{3,2,1,0:T(8,128)(2,1)S(1)}, u32[]{:S(2)}) copy-start(bf16[16,2,128,128]{3,2,1,0:T(8,128)(2,1)S(1)} %collective-permute-done.1.sh2) | copy-start | bytes 3145732
  51.9 31.3 %collective-permute-start.2 = (bf16[16,2,128,128]{3,2,1,0:T(8,128)(2,1)S(1)}, bf16[16,2,128,128]{3,2,1,0:T(8,128)(2,1)}, u32[]{:S(2)}, u32[]{:S(2)}) collective-permute-start(bf16[16,2,128,128]{3,2,1,0:T(8,128)(2,1)S(1)} %collective-permute-done.1.sh2), channel_id=1, source_target_pairs={{0,1},{1,0},{2,3},{3,2},{4,5},{5,4},{6,7},{7,6},{8,9},{9,8},{10,11... | collective-permute-start | bytes 3145736 | tf_op jit(solution)/shard_map/ppermute | solution.py:249
  61.2 22.0 %all-to-all-start.1 = ((bf16[128,16,256]{2,0,1:T(8,128)(2,1)}), bf16[128,16,256]{2,0,1:T(8,128)(2,1)S(1)}, u32[]{:S(2)}, u32[]{:S(2)}) async-start(bf16[128,16,256]{2,0,1:T(8,128)(2,1)} %bitcast.26), calls=%async_computation.1 | async-start | bytes 2097152 | tf_op jit(solution)/shard_map/all_to_all | solution.py:252
  83.2 1.0 copy-start.3

commit v2 on v1

--- a/solution.py
+++ b/solution.py
@@ -23,26 +23,31 @@
 
 
 def attn_kernel(
-    tab, q_in, own, swp, pas, sh2, vkv, o_ref, q_ref, ks, vs, bias, s0, s1, m0, m1, p0, p1, l0, l1, sem, sem1
+    tab, qk2, v2, own, swp, pk, pv, vkv, o_ref, q_ref, ks, vs, bias, s0, s1, m0, m1, p0, p1, l0, l1, sem, sem1
 ):
     run = tab[0]
     odd = (run & 1) == 1
-    copies = [pltpu.make_async_copy(q_in, q_ref, sem.at[0])]
-    for n, part in enumerate((ks, vs)):
-        for m, src in ((0, sh2), (2, own)):
-            copies.append(
-                pltpu.make_async_copy(src.at[:, n], part.at[pl.ds(m * 16, 16)], sem.at[1 + 2 * n + m // 2])
-            )
-        copies.append(pltpu.make_async_copy(vkv.at[n], part.at[pl.ds(48, NSLOT // 2)], sem.at[5 + n]))
+    copies = []
+    for src, dst in (
+        (qk2.at[:, 0], q_ref.at[0]),
+        (qk2.at[:, 1], q_ref.at[1]),
+        (qk2.at[:, 2], ks.at[pl.ds(0, 16)]),
+        (v2, vs.at[pl.ds(0, 16)]),
+        (own.at[:, 0], ks.at[pl.ds(32, 16)]),
+        (own.at[:, 1], vs.at[pl.ds(32, 16)]),
+        (vkv.at[0], ks.at[pl.ds(48, NSLOT // 2)]),
+        (vkv.at[1], vs.at[pl.ds(48, NSLOT // 2)]),
+    ):
+        copies.append(pltpu.make_async_copy(src, dst, sem.at[len(copies)]))
     for c in copies:
         c.start()
-    for cond, src in ((odd, swp), (jnp.logical_not(odd), pas)):
+    for cond, srcs in ((odd, (swp.at[:, 0], swp.at[:, 1])), (jnp.logical_not(odd), (pk, pv))):
 
         @pl.when(cond)
         def _():
             both = [
-                pltpu.make_async_copy(src.at[:, n], part.at[pl.ds(16, 16)], sem1.at[n])
-                for n, part in enumerate((ks, vs))
+                pltpu.make_async_copy(src, part.at[pl.ds(16, 16)], sem1.at[n])
+                for n, (src, part) in enumerate(zip(srcs, (ks, vs)))
             ]
             for c in both:
                 c.start()
@@ -83,6 +88,7 @@
     maxima = (m0, m1)
     probs = (p0, p1)
     totals = (l0, l1)
+    queries = q_ref.reshape(2, NBD * BLK, HD)
     ksv = ks.reshape(52 * 128, HD)
     vsv = vs.reshape(52 * 128, HD)
 
@@ -100,7 +106,7 @@
             il = t * (G // 2) + g // 2
             hh = g % 2
             row = pl.multiple_of(il * BLK, BLK)
-            q = q_ref[pl.ds(row, BLK), hh * HD : (hh + 1) * HD]
+            q = queries[hh, pl.ds(row, BLK), :]
             m = None
             for c0 in range(0, 7, CH):
                 cs = list(range(c0, min(7, c0 + CH)))
@@ -153,17 +159,17 @@
     lax.fori_loop(0, steps // 2, body, 0)
 
 
-def attend(tab, q, own, swp, pas, sh2, vkv):
+def attend(tab, qk2, v2, own, swp, pk, pv, vkv):
     hbm = pl.BlockSpec(memory_space=pl.ANY)
     smem = pl.BlockSpec(memory_space=pltpu.SMEM)
     vmem = pl.BlockSpec(memory_space=pltpu.VMEM)
     return pl.pallas_call(
         attn_kernel,
         out_shape=jax.ShapeDtypeStruct((NBD * BLK, 2 * HD), jnp.bfloat16),
-        in_specs=[smem] + [hbm] * 6,
+        in_specs=[smem] + [hbm] * 7,
         out_specs=vmem,
         scratch_shapes=[
-            pltpu.VMEM((NBD * BLK, 2 * HD), jnp.bfloat16),
+            pltpu.VMEM((2, 16, 128, HD), jnp.bfloat16),
             pltpu.VMEM((52, 128, HD), jnp.bfloat16),
             pltpu.VMEM((52, 128, HD), jnp.bfloat16),
             pltpu.VMEM((2 * NBD, 8, 896), jnp.float32),
@@ -175,12 +181,12 @@
             pltpu.VMEM((G, BLK, 896), jnp.bfloat16),
             pltpu.VMEM((G, BLK, 128), jnp.float32),
             pltpu.VMEM((G, BLK, 128), jnp.float32),
-            pltpu.SemaphoreType.DMA((7,)),
+            pltpu.SemaphoreType.DMA((8,)),
             pltpu.SemaphoreType.DMA((2,)),
         ],
         cost_estimate=pl.CostEstimate(flops=2_000_000_000, bytes_accessed=6_000_000, transcendentals=4_000_000),
         name="attend",
-    )(tab, q, own, swp, pas, sh2, vkv)
+    )(tab, qk2, v2, own, swp, pk, pv, vkv)
 
 
 def pick_kernel(tab, kv, o_ref):
@@ -222,6 +228,25 @@
     return jnp.concatenate([p.astype(jnp.int32) for p in parts])
 
 
+def pack_kernel(q, k, o_ref):
+    for d in range(16):
+        for n in range(2):
+            o_ref[d, n] = q[:, (2 * d + n) * HD : (2 * d + n + 1) * HD]
+        o_ref[d, 2] = k[:, d // 2 * HD : (d // 2 + 1) * HD]
+
+
+def pack(q, k):
+    vmem = pl.BlockSpec(memory_space=pltpu.VMEM)
+    return pl.pallas_call(
+        pack_kernel,
+        out_shape=jax.ShapeDtypeStruct((16, 3, 128, HD), jnp.bfloat16),
+        in_specs=[vmem, vmem],
+        out_specs=vmem,
+        cost_estimate=pl.CostEstimate(flops=0, bytes_accessed=3_000_000, transcendentals=0),
+        name="pack",
+    )(q, k)
+
+
 def by_head(k, v):
     rows = k.shape[0]
     k3 = k.reshape(rows, KVH, HD).transpose(1, 0, 2)
@@ -241,16 +266,20 @@
     swap = [(r, r ^ 1) for r in range(runs)]
     tab = table(vertical_blocks, slash_offsets, head, run)
     own = exchange(by_head(key_states, value_states), "head")
+    k2 = lax.ppermute(key_states, "qblk", ahead)
+    qk2 = pack(queries, k2)
     own, tab = lax.optimization_barrier((own, tab))
     cand = pick(tab, own).reshape(runs, NSLOT * 128 // runs, HD)
     cand = exchange(cand, "qblk")
-    sh2 = lax.ppermute(own, "qblk", ahead)
+    v_own = own[:, 1]
+    v2 = lax.ppermute(v_own, "qblk", ahead)
     swp = lax.ppermute(own, "qblk", swap)
-    pas = lax.ppermute(sh2, "qblk", swap)
+    pv = lax.ppermute(v2, "qblk", swap)
     part = jnp.sum(cand.astype(jnp.float32), axis=0).astype(jnp.bfloat16)
     vert = lax.all_gather(part, "qblk", axis=0, tiled=True)
-    q = lax.all_to_all(queries, "head", split_axis=1, concat_axis=0, tiled=True)
-    out = attend(tab, q, own, swp, pas, sh2, vert.reshape(2, NSLOT // 2, 128, HD))
+    qk2 = exchange(qk2, "head")
+    pk = lax.ppermute(qk2[:, 2], "qblk", swap)
+    out = attend(tab, qk2, v2, own, swp, pk, pv, vert.reshape(2, NSLOT // 2, 128, HD))
     return lax.all_to_all(out, "head", split_axis=0, concat_axis=1, tiled=True)
 
 

time: 125 us -> 129 us (1.032)
  waiting for transfers between devices: 27 us -> 31.9 us
  blocking collectives: 40.8 us -> 36.1 us
  Pallas kernels: 18.1 us -> 20.8 us
  starting transfers between devices: 30.7 us -> 32.3 us
    ppermute x2 -> x4, waiting for transfers between devices: 11.4 us -> 18 us  [the longest x1 9.59 us: per_device(): k2 = lax.ppermute(key_states, 'qblk', ahead)]
    all_to_all x2 -> x3, starting transfers between devices: 18.6 us -> 23.7 us  [exchange(): return lax.all_to_all(x, axis, split_axis=0, concat_axis=0, tiled=True)]
    all_to_all x1 -> x0, starting transfers between devices: 3.89 us -> none  [per_device(): q = lax.all_to_all(queries, 'head', split_axis=1, concat_axis=0, tiled=True)]
    all_to_all x1, blocking collectives: 22.7 us -> 19.5 us  [per_device(): return lax.all_to_all(out, 'head', split_axis=0, concat_axis=1, tiled=True)]
    ppermute x1, starting transfers between devices: 0.19 us -> 3.13 us  [per_device(): swp = lax.ppermute(own, 'qblk', swap)]
    pallas_call x0 -> x1, Pallas kernels: none -> 2.67 us  [pack(): pl.pallas_call(pack_kernel, out_shape=jax.ShapeDtypeStruct((16, 3, 128, H...]
    ppermute x2 -> x4, starting transfers between devices: 8.06 us -> 5.47 us  [the longest x1 3.43 us: per_device(): pv = lax.ppermute(v2, 'qblk', swap)]
    all_to_all x2 -> x3, waiting for transfers between devices: 15.6 us -> 13.9 us  [exchange(): return lax.all_to_all(x, axis, split_axis=0, concat_axis=0, tiled=True)]
  transfers between devices with their start and end apart: 6 -> 8, of which waited for: 3 -> 5; matrix products, arithmetic and copies ran while one was open for 2% -> 1% of each run, Pallas kernels for 2% -> 4%
where the time goes in v2:
time: 129 us; the launch traced here: 128 us
  blocking collectives  36.1 us (28%)
  starting transfers between devices  32.3 us (25%)
  waiting for transfers between devices  31.9 us (25%)
  Pallas kernels  20.8 us (16%)
  local copies, waits for them, and re-layouts  6.48 us (5%)
    all_to_all x3, starting transfers between devices, exchange(): return lax.all_to_all(x, axis, split_axis=0, concat_axis=0, tiled=True)  23.7 us
    all_to_all x1, blocking collectives, per_device(): return lax.all_to_all(out, 'head', split_axis=0, concat_axis=1, tiled=True)  19.5 us
    all_gather x1, blocking collectives, per_device(): vert = lax.all_gather(part, 'qblk', axis=0, tiled=True)  16.6 us
    pallas_call x1, Pallas kernels, attend(): pl.pallas_call(attn_kernel, out_shape=jax.ShapeDtypeStruct((NBD * BLK, 2...  16.2 us
    all_to_all x3, waiting for transfers between devices, exchange(): return lax.all_to_all(x, axis, split_axis=0, concat_axis=0, tiled=True)  13.9 us
    ppermute x1, waiting for transfers between devices, per_device(): k2 = lax.ppermute(key_states, 'qblk', ahead)  9.59 us
    ppermute x1, waiting for transfers between devices, per_device(): v2 = lax.ppermute(v_own, 'qblk', ahead)  8.36 us
    ppermute x1, starting transfers between devices, per_device(): pv = lax.ppermute(v2, 'qblk', swap)  3.43 us
  transfers between devices with their start and end apart: 8, of which 5 were waited for; matrix products, arithmetic and copies ran while one was open for 1% of the time, Pallas kernels for 4%

profile of v2, /device:TPU:1, one launch (start us, length us, event | category | flops | bytes accessed | tf_op | source)
XLA Modules:
  0.0 128.5 jit_solution(15338025215982085813)
XLA Ops:
  0.0 1.0 copy.30
  1.0 1.0 copy.29
  2.2 1.3 broadcast_in_dim.38
  3.5 7.6 %all-to-all-start = ((bf16[16,2,128,128]{3,2,1,0:T(8,128)(2,1)}), bf16[16,2,128,128]{3,2,1,0:T(8,128)(2,1)S(1)}, u32[]{:S(2)}, u32[]{:S(2)}) async-start(bf16[16,2,128,128]{3,2,1,0:T(8,128)(2,1)} %bitcast.4), calls=%async_computation | async-start | bytes 2097152 | tf_op jit(solution)/shard_map/all_to_all | solution.py:258
  11.1 1.7 %collective-permute-start = (bf16[128,1024]{1,0:T(8,128)(2,1)S(1)}, bf16[128,1024]{1,0:T(8,128)(2,1)S(1)}, u32[]{:S(2)}, u32[]{:S(2)}) collective-permute-start(bf16[128,1024]{1,0:T(8,128)(2,1)S(1)} %copy-done.3), channel_id=1, source_target_pairs={{0,2},{1,3},{2,4},{3,5},{4,6},{5,7},{6,8},{7,9},{8,10},{9,11},{10,... | collective-permute-start | bytes 786440 | tf_op jit(solution)/shard_map/ppermute | solution.py:269
  12.9 9.6 %collective-permute-done.k = bf16[128,1024]{1,0:T(8,128)(2,1)S(1)} collective-permute-done((bf16[128,1024]{1,0:T(8,128)(2,1)S(1)}, bf16[128,1024]{1,0:T(8,128)(2,1)S(1)}, u32[]{:S(2)}, u32[]{:S(2)}) %collective-permute-start) | collective-permute-done | bytes 262176 | tf_op jit(solution)/shard_map/ppermute | solution.py:269
  22.5 0.7 copy-done.4
  23.2 2.7 %pack.1 = bf16[16,3,128,128]{3,2,1,0:T(8,128)(2,1)} custom-call(bf16[128,4096]{1,0:T(8,128)(2,1)} %q.1, bf16[128,1024]{1,0:T(8,128)(2,1)} %copy-done.4), custom_call_target="tpu_custom_call" | custom-call | bytes 3000000 | tf_op jit(solution)/shard_map/pack/pallas_call | solution.py:240
  25.8 0.9 all-to-all-done.kv.own
  26.7 5.5 %all-to-all-start.1 = ((bf16[16,3,128,128]{3,2,1,0:T(8,128)(2,1)}), bf16[16,3,128,128]{3,2,1,0:T(8,128)(2,1)S(1)}, u32[]{:S(2)}, u32[]{:S(2)}) async-start(bf16[16,3,128,128]{3,2,1,0:T(8,128)(2,1)} %pack.1), calls=%async_computation.1 | async-start | bytes 3145728 | tf_op jit(solution)/shard_map/all_to_all | solution.py:258
  33.2 0.2 select_reduce_fusion.1
  33.4 0.6 concatenate.3.tab
  34.1 3.1 %collective-permute-start.2 = (bf16[16,2,128,128]{3,2,1,0:T(8,128)(2,1)S(1)}, bf16[16,2,128,128]{3,2,1,0:T(8,128)(2,1)}, u32[]{:S(2)}, u32[]{:S(2)}) collective-permute-start(bf16[16,2,128,128]{3,2,1,0:T(8,128)(2,1)S(1)} %all-to-all-done.kv.own), channel_id=1, source_target_pairs={{0,1},{1,0},{2,3},{3,2},{4,5},{5,4},{6,7},{7,6},{8,9},{9,8},{10,11... | collective-permute-start | bytes 3145736 | tf_op jit(solution)/shard_map/ppermute | solution.py:276
  37.3 2.0 %pick.1 = bf16[1024,128]{1,0:T(8,128)(2,1)} custom-call(s32[40]{0:T(128)} %concatenate.3.tab, bf16[16,2,128,128]{3,2,1,0:T(8,128)(2,1)} %copy-done.1), custom_call_target="tpu_custom_call" | custom-call | flops 1000000 | bytes 1500000 | tf_op jit(solution)/shard_map/pick/pallas_call | solution.py:207
  39.3 8.4 %collective-permute-done.1.v2 = bf16[16,128,128]{2,1,0:T(8,128)(2,1)} collective-permute-done((bf16[16,128,128]{2,1,0:T(8,128)(2,1)S(1)}, bf16[16,128,128]{2,1,0:T(8,128)(2,1)}, u32[]{:S(2)}, u32[]{:S(2)}) %collective-permute-start.1) | collective-permute-done | bytes 524320 | tf_op jit(solution)/shard_map/ppermute | solution.py:275
  47.6 3.4 %collective-permute-start.4 = (bf16[16,128,128]{2,1,0:T(8,128)(2,1)}, bf16[16,128,128]{2,1,0:T(8,128)(2,1)}, u32[]{:S(2)}, u32[]{:S(2)}) collective-permute-start(bf16[16,128,128]{2,1,0:T(8,128)(2,1)} %collective-permute-done.1.v2), channel_id=1, source_target_pairs={{0,1},{1,0},{2,3},{3,2},{4,5},{5,4},{6,7},{7,6},{8,9},{9,8},{10,11... | collective-permute-start | bytes 1572872 | tf_op jit(solution)/shard_map/ppermute | solution.py:277
  51.1 1.7 %all-to-all-done.1.qk2 = bf16[16,3,128,128]{3,2,1,0:T(8,128)(2,1)S(1)} async-done(((bf16[16,3,128,128]{3,2,1,0:T(8,128)(2,1)}), bf16[16,3,128,128]{3,2,1,0:T(8,128)(2,1)S(1)}, u32[]{:S(2)}, u32[]{:S(2)}) %all-to-all-start.1) | async-done | bytes 1572896 | tf_op jit(solution)/shard_map/all_to_all | solution.py:258
  52.7 10.7 %all-to-all-start.2 = ((bf16[16,64,128]{2,1,0:T(8,128)(2,1)}), bf16[16,64,128]{2,1,0:T(8,128)(2,1)S(1)}, u32[]{:S(2)}, u32[]{:S(2)}) async-start(bf16[16,64,128]{2,1,0:T(8,128)(2,1)} %bitcast.28), calls=%async_computation.2 | async-start | bytes 524288 | tf_op jit(solution)/shard_map/all_to_all | solution.py:258
  63.5 0.2 collective-permute-start.3
  63.7 11.3 %all-to-all-done.2 = bf16[16,64,128]{2,1,0:T(8,128)(2,1)S(1)} async-done(((bf16[16,64,128]{2,1,0:T(8,128)(2,1)}), bf16[16,64,128]{2,1,0:T(8,128)(2,1)S(1)}, u32[]{:S(2)}, u32[]{:S(2)}) %all-to-all-start.2) | async-done | bytes 262176 | tf_op jit(solution)/shard_map/all_to_all | solution.py:258
  75.1 16.6 %all_gather.3 = bf16[1024,128]{1,0:T(8,128)(2,1)} all-gather(bf16[64,128]{1,0:T(8,128)(2,1)S(1)} %reduce_sum.42), channel_id=1, replica_groups=mesh['head'=16,'qblk'=16] {'qblk'}, dimensions={0}, use_global_device_ids=true | all-gather | bytes 278528 | tf_op jit(solution)/shard_map/all_gather | solution.py:279
  91.7 16.2 %attend.1 = bf16[2048,256]{1,0:T(8,128)(2,1)} custom-call(s32[40]{0:T(128)} %concatenate.3.tab, bf16[16,3,128,128]{3,2,1,0:T(8,128)(2,1)} %copy-done.2, bf16[16,128,128]{2,1,0:T(8,128)(2,1)} %collective-permute-done.1.v2, bf16[16,2,128,128]{3,2,1,0:T(8,128)(2,1)} %copy-done.1, bf16[16,2,128,128]{3,2,1,0:T(8,128)(2,1)} %collective-permute-done.2.swp, ...), custom_call_target="tpu_custom_call" | custom-call | flops 2000000000 | bytes 6000000 | tf_op jit(solution)/shard_map/attend/pallas_call | solution.py:166
  107.9 19.5 %all_to_all.34 = bf16[16,128,256]{2,1,0:T(8,128)(2,1)S(1)} all-to-all(bf16[16,128,256]{2,1,0:T(8,128)(2,1)} %bitcast.29), channel_id=1, replica_groups=mesh['head'=16,'qblk'=16] {'head'}, dimensions={0} | all-to-all | bytes 2097152 | tf_op jit(solution)/shard_map/all_to_all | solution.py:283
  127.4 1.1 copy.28
  (32 shorter events, 1.5 us)
Async XLA Ops:
  0.0 32.8 %copy-start = (s32[32,8]{0,1:T(8,128)S(1)}, s32[32,8]{0,1:T(8,128)}, u32[]{:S(2)}) copy-start(s32[32,8]{0,1:T(8,128)} %param.9) | copy-start | bytes 3076
  2.2 8.9 %copy-start.3 = (bf16[128,1024]{1,0:T(8,128)(2,1)S(1)}, bf16[128,1024]{1,0:T(8,128)(2,1)}, u32[]{:S(2)}) copy-start(bf16[128,1024]{1,0:T(8,128)(2,1)} %param.6) | copy-start | bytes 786436
  2.2 10.6 %copy-start.5 = (s32[32,5]{0,1:T(8,128)S(1)}, s32[32,5]{0,1:T(8,128)}, u32[]{:S(2)}) copy-start(s32[32,5]{0,1:T(8,128)} %param.8) | copy-start | bytes 1924
  3.5 23.2 %all-to-all-start = ((bf16[16,2,128,128]{3,2,1,0:T(8,128)(2,1)}), bf16[16,2,128,128]{3,2,1,0:T(8,128)(2,1)S(1)}, u32[]{:S(2)}, u32[]{:S(2)}) async-start(bf16[16,2,128,128]{3,2,1,0:T(8,128)(2,1)} %bitcast.4), calls=%async_computation | async-start | bytes 2097152 | tf_op jit(solution)/shard_map/all_to_all | solution.py:258
  11.1 11.4 %collective-permute-start = (bf16[128,1024]{1,0:T(8,128)(2,1)S(1)}, bf16[128,1024]{1,0:T(8,128)(2,1)S(1)}, u32[]{:S(2)}, u32[]{:S(2)}) collective-permute-start(bf16[128,1024]{1,0:T(8,128)(2,1)S(1)} %copy-done.3), channel_id=1, source_target_pairs={{0,2},{1,3},{2,4},{3,5},{4,6},{5,7},{6,8},{7,9},{8,10},{9,11},{10,... | collective-permute-start | bytes 786440 | tf_op jit(solution)/shard_map/ppermute | solution.py:269
  22.5 0.7 copy-start.4
  26.7 7.4 %copy-start.1 = (bf16[16,2,128,128]{3,2,1,0:T(8,128)(2,1)}, bf16[16,2,128,128]{3,2,1,0:T(8,128)(2,1)S(1)}, u32[]{:S(2)}) copy-start(bf16[16,2,128,128]{3,2,1,0:T(8,128)(2,1)S(1)} %all-to-all-done.kv.own) | copy-start | bytes 3145732
  26.7 26.0 %all-to-all-start.1 = ((bf16[16,3,128,128]{3,2,1,0:T(8,128)(2,1)}), bf16[16,3,128,128]{3,2,1,0:T(8,128)(2,1)S(1)}, u32[]{:S(2)}, u32[]{:S(2)}) async-start(bf16[16,3,128,128]{3,2,1,0:T(8,128)(2,1)} %pack.1), calls=%async_computation.1 | async-start | bytes 3145728 | tf_op jit(solution)/shard_map/all_to_all | solution.py:258
  34.0 13.6 %collective-permute-start.1 = (bf16[16,128,128]{2,1,0:T(8,128)(2,1)S(1)}, bf16[16,128,128]{2,1,0:T(8,128)(2,1)}, u32[]{:S(2)}, u32[]{:S(2)}) collective-permute-start(bf16[16,128,128]{2,1,0:T(8,128)(2,1)S(1)} %slice_bitcast_fusion.1), channel_id=1, source_target_pairs={{0,2},{1,3},{2,4},{3,5},{4,6},{5,7},{6,8},{7,9},{8,10},{9,11},{10,... | collective-permute-start | bytes 1572872 | tf_op jit(solution)/shard_map/ppermute | solution.py:275
  34.1 57.5 %collective-permute-start.2 = (bf16[16,2,128,128]{3,2,1,0:T(8,128)(2,1)S(1)}, bf16[16,2,128,128]{3,2,1,0:T(8,128)(2,1)}, u32[]{:S(2)}, u32[]{:S(2)}) collective-permute-start(bf16[16,2,128,128]{3,2,1,0:T(8,128)(2,1)S(1)} %all-to-all-done.kv.own), channel_id=1, source_target_pairs={{0,1},{1,0},{2,3},{3,2},{4,5},{5,4},{6,7},{7,6},{8,9},{9,8},{10,11... | collective-permute-start | bytes 3145736 | tf_op jit(solution)/shard_map/ppermute | solution.py:276
  47.6 44.0 %collective-permute-start.4 = (bf16[16,128,128]{2,1,0:T(8,128)(2,1)}, bf16[16,128,128]{2,1,0:T(8,128)(2,1)}, u32[]{:S(2)}, u32[]{:S(2)}) collective-permute-start(bf16[16,128,128]{2,1,0:T(8,128)(2,1)} %collective-permute-done.1.v2), channel_id=1, source_target_pairs={{0,1},{1,0},{2,3},{3,2},{4,5},{5,4},{6,7},{7,6},{8,9},{9,8},{10,11... | collective-permute-start | bytes 1572872 | tf_op jit(solution)/shard_map/ppermute | solution.py:277
  52.7 38.9 %copy-start.2 = (bf16[16,3,128,128]{3,2,1,0:T(8,128)(2,1)}, bf16[16,3,128,128]{3,2,1,0:T(8,128)(2,1)S(1)}, u32[]{:S(2)}) copy-start(bf16[16,3,128,128]{3,2,1,0:T(8,128)(2,1)S(1)} %all-to-all-done.1.qk2) | copy-start | bytes 4718596
  52.7 22.3 %all-to-all-start.2 = ((bf16[16,64,128]{2,1,0:T(8,128)(2,1)}), bf16[16,64,128]{2,1,0:T(8,128)(2,1)S(1)}, u32[]{:S(2)}, u32[]{:S(2)}) async-start(bf16[16,64,128]{2,1,0:T(8,128)(2,1)} %bitcast.28), calls=%async_computation.2 | async-start | bytes 524288 | tf_op jit(solution)/shard_map/all_to_all | solution.py:258
  63.5 28.2 %collective-permute-start.3 = (bf16[16,128,128]{2,1,0:T(8,128)(2,1)S(1)}, bf16[16,128,128]{2,1,0:T(8,128)(2,1)}, u32[]{:S(2)}, u32[]{:S(2)}) collective-permute-start(bf16[16,128,128]{2,1,0:T(8,128)(2,1)S(1)} %slice_bitcast_fusion), channel_id=1, source_target_pairs={{0,1},{1,0},{2,3},{3,2},{4,5},{5,4},{6,7},{7,6},{8,9},{9,8},{10,11... | collective-permute-start | bytes 1572872 | tf_op jit(solution)/shard_map/ppermute | solution.py:281

commit v3 on v2

--- a/solution.py
+++ b/solution.py
@@ -6,7 +6,6 @@
 from jax.sharding import PartitionSpec as P
 
 
-KVH = 8
 HD = 128
 BLK = 64
 NV = 5
@@ -51,8 +50,6 @@
             ]
             for c in both:
                 c.start()
-            for c in both:
-                c.wait()
 
     lane = lax.broadcasted_iota(jnp.int32, (8, 128), 1)
     slash = [[tab[19 + hh * NS + n] for n in range(NS)] for hh in range(2)]
@@ -80,6 +77,8 @@
     lax.fori_loop(0, NBD, mask, 0, unroll=4)
     for c in copies:
         c.wait()
+    for n, (src, part) in enumerate(((pk, ks), (pv, vs))):
+        pltpu.make_async_copy(src, part.at[pl.ds(16, 16)], sem1.at[n]).wait()
 
     rr = lax.broadcasted_iota(jnp.int32, (BLK, 128), 0)
     cc = lax.broadcasted_iota(jnp.int32, (BLK, 128), 1)
@@ -247,11 +246,22 @@
     )(q, k)
 
 
-def by_head(k, v):
-    rows = k.shape[0]
-    k3 = k.reshape(rows, KVH, HD).transpose(1, 0, 2)
-    v3 = v.reshape(rows, KVH, HD).transpose(1, 0, 2)
-    return jnp.repeat(jnp.stack([k3, v3], axis=1), 2, axis=0)
+def pair_kernel(k, v, o_ref):
+    for d in range(16):
+        for n, x in enumerate((k, v)):
+            o_ref[d, n] = x[:, d // 2 * HD : (d // 2 + 1) * HD]
+
+
+def pair(k, v):
+    vmem = pl.BlockSpec(memory_space=pltpu.VMEM)
+    return pl.pallas_call(
+        pair_kernel,
+        out_shape=jax.ShapeDtypeStruct((16, 2, 128, HD), jnp.bfloat16),
+        in_specs=[vmem, vmem],
+        out_specs=vmem,
+        cost_estimate=pl.CostEstimate(flops=0, bytes_accessed=2_000_000, transcendentals=0),
+        name="pair",
+    )(k, v)
 
 
 def exchange(x, axis):
@@ -265,7 +275,8 @@
     ahead = [(r, (r + 2) % runs) for r in range(runs)]
     swap = [(r, r ^ 1) for r in range(runs)]
     tab = table(vertical_blocks, slash_offsets, head, run)
-    own = exchange(by_head(key_states, value_states), "head")
+    kv = pair(key_states, value_states)
+    own = exchange(kv, "head")
     k2 = lax.ppermute(key_states, "qblk", ahead)
     qk2 = pack(queries, k2)
     own, tab = lax.optimization_barrier((own, tab))

time: 129 us -> 127 us (0.984)
  local copies, waits for them, and re-layouts: 6.48 us -> 3.1 us
    pallas_call x0 -> x1, Pallas kernels: none -> 2.18 us  [pair(): pl.pallas_call(pair_kernel, out_shape=jax.ShapeDtypeStruct((16, 2, 128, H...]
    unnamed x14 -> x12, local copies, waits for them, and re-layouts: 2.72 us -> 0.72 us
  transfers between devices with their start and end apart: 8 -> 8, of which waited for: 5 -> 5; matrix products, arithmetic and copies ran while one was open for 1% -> 2% of each run, Pallas kernels for 4% -> 4%
where the time goes in v3:
time: 127 us; the launch traced here: 126 us
  blocking collectives  36.1 us (28%)
  starting transfers between devices  32.4 us (26%)
  waiting for transfers between devices  31.9 us (25%)
  Pallas kernels  22 us (17%)
  local copies, waits for them, and re-layouts  3.1 us (2%)
    all_to_all x3, starting transfers between devices, exchange(): return lax.all_to_all(x, axis, split_axis=0, concat_axis=0, tiled=True)  23.7 us
    all_to_all x1, blocking collectives, per_device(): return lax.all_to_all(out, 'head', split_axis=0, concat_axis=1, tiled=True)  19.5 us
    all_gather x1, blocking collectives, per_device(): vert = lax.all_gather(part, 'qblk', axis=0, tiled=True)  16.6 us
    pallas_call x1, Pallas kernels, attend(): pl.pallas_call(attn_kernel, out_shape=jax.ShapeDtypeStruct((NBD * BLK, 2...  15.2 us
    all_to_all x3, waiting for transfers between devices, exchange(): return lax.all_to_all(x, axis, split_axis=0, concat_axis=0, tiled=True)  13.9 us
    ppermute x1, waiting for transfers between devices, per_device(): k2 = lax.ppermute(key_states, 'qblk', ahead)  9.59 us
    ppermute x1, waiting for transfers between devices, per_device(): v2 = lax.ppermute(v_own, 'qblk', ahead)  8.36 us
    ppermute x1, starting transfers between devices, per_device(): pv = lax.ppermute(v2, 'qblk', swap)  3.43 us
  transfers between devices with their start and end apart: 8, of which 5 were waited for; matrix products, arithmetic and copies ran while one was open for 2% of the time, Pallas kernels for 4%

profile of v3, /device:TPU:1, one launch (start us, length us, event | category | flops | bytes accessed | tf_op | source)
XLA Modules:
  0.0 126.2 jit_solution(1054703506749178574)
XLA Ops:
  0.0 2.2 %pair.1 = bf16[16,2,128,128]{3,2,1,0:T(8,128)(2,1)} custom-call(bf16[128,1024]{1,0:T(8,128)(2,1)} %k.1, bf16[128,1024]{1,0:T(8,128)(2,1)} %v.1), custom_call_target="tpu_custom_call" | custom-call | bytes 2000000 | tf_op jit(solution)/shard_map/pair/pallas_call | solution.py:257
  2.2 7.6 %all-to-all-start = ((bf16[16,2,128,128]{3,2,1,0:T(8,128)(2,1)}), bf16[16,2,128,128]{3,2,1,0:T(8,128)(2,1)S(1)}, u32[]{:S(2)}, u32[]{:S(2)}) async-start(bf16[16,2,128,128]{3,2,1,0:T(8,128)(2,1)} %pair.1), calls=%async_computation | async-start | bytes 2097152 | tf_op jit(solution)/shard_map/all_to_all | solution.py:268
  9.8 1.7 %collective-permute-start = (bf16[128,1024]{1,0:T(8,128)(2,1)S(1)}, bf16[128,1024]{1,0:T(8,128)(2,1)S(1)}, u32[]{:S(2)}, u32[]{:S(2)}) collective-permute-start(bf16[128,1024]{1,0:T(8,128)(2,1)S(1)} %copy-done.3), channel_id=1, source_target_pairs={{0,2},{1,3},{2,4},{3,5},{4,6},{5,7},{6,8},{7,9},{8,10},{9,11},{10,... | collective-permute-start | bytes 786440 | tf_op jit(solution)/shard_map/ppermute | solution.py:280
  11.6 9.6 %collective-permute-done.k = bf16[128,1024]{1,0:T(8,128)(2,1)S(1)} collective-permute-done((bf16[128,1024]{1,0:T(8,128)(2,1)S(1)}, bf16[128,1024]{1,0:T(8,128)(2,1)S(1)}, u32[]{:S(2)}, u32[]{:S(2)}) %collective-permute-start) | collective-permute-done | bytes 262176 | tf_op jit(solution)/shard_map/ppermute | solution.py:280
  21.2 0.7 copy-done.4
  21.9 2.7 %pack.1 = bf16[16,3,128,128]{3,2,1,0:T(8,128)(2,1)} custom-call(bf16[128,4096]{1,0:T(8,128)(2,1)} %q.1, bf16[128,1024]{1,0:T(8,128)(2,1)} %copy-done.4), custom_call_target="tpu_custom_call" | custom-call | bytes 3000000 | tf_op jit(solution)/shard_map/pack/pallas_call | solution.py:239
  24.5 0.9 all-to-all-done.kv.own
  25.4 5.5 %all-to-all-start.1 = ((bf16[16,3,128,128]{3,2,1,0:T(8,128)(2,1)}), bf16[16,3,128,128]{3,2,1,0:T(8,128)(2,1)S(1)}, u32[]{:S(2)}, u32[]{:S(2)}) async-start(bf16[16,3,128,128]{3,2,1,0:T(8,128)(2,1)} %pack.1), calls=%async_computation.1 | async-start | bytes 3145728 | tf_op jit(solution)/shard_map/all_to_all | solution.py:268
  30.9 0.2 slice_reduce_fusion
  31.2 0.2 compare_reduce_fusion
  31.9 0.2 select_reduce_fusion.1
  32.1 0.6 concatenate.3.tab
  32.8 3.1 %collective-permute-start.2 = (bf16[16,2,128,128]{3,2,1,0:T(8,128)(2,1)S(1)}, bf16[16,2,128,128]{3,2,1,0:T(8,128)(2,1)}, u32[]{:S(2)}, u32[]{:S(2)}) collective-permute-start(bf16[16,2,128,128]{3,2,1,0:T(8,128)(2,1)S(1)} %all-to-all-done.kv.own), channel_id=1, source_target_pairs={{0,1},{1,0},{2,3},{3,2},{4,5},{5,4},{6,7},{7,6},{8,9},{9,8},{10,11... | collective-permute-start | bytes 3145736 | tf_op jit(solution)/shard_map/ppermute | solution.py:287
  36.0 2.0 %pick.1 = bf16[1024,128]{1,0:T(8,128)(2,1)} custom-call(s32[40]{0:T(128)} %concatenate.3.tab, bf16[16,2,128,128]{3,2,1,0:T(8,128)(2,1)} %copy-done.1), custom_call_target="tpu_custom_call" | custom-call | flops 1000000 | bytes 1500000 | tf_op jit(solution)/shard_map/pick/pallas_call | solution.py:206
  38.0 8.4 %collective-permute-done.1.v2 = bf16[16,128,128]{2,1,0:T(8,128)(2,1)} collective-permute-done((bf16[16,128,128]{2,1,0:T(8,128)(2,1)S(1)}, bf16[16,128,128]{2,1,0:T(8,128)(2,1)}, u32[]{:S(2)}, u32[]{:S(2)}) %collective-permute-start.1) | collective-permute-done | bytes 524320 | tf_op jit(solution)/shard_map/ppermute | solution.py:286
  46.3 3.4 %collective-permute-start.4 = (bf16[16,128,128]{2,1,0:T(8,128)(2,1)}, bf16[16,128,128]{2,1,0:T(8,128)(2,1)}, u32[]{:S(2)}, u32[]{:S(2)}) collective-permute-start(bf16[16,128,128]{2,1,0:T(8,128)(2,1)} %collective-permute-done.1.v2), channel_id=1, source_target_pairs={{0,1},{1,0},{2,3},{3,2},{4,5},{5,4},{6,7},{7,6},{8,9},{9,8},{10,11... | collective-permute-start | bytes 1572872 | tf_op jit(solution)/shard_map/ppermute | solution.py:288
  49.8 1.7 %all-to-all-done.1.qk2 = bf16[16,3,128,128]{3,2,1,0:T(8,128)(2,1)S(1)} async-done(((bf16[16,3,128,128]{3,2,1,0:T(8,128)(2,1)}), bf16[16,3,128,128]{3,2,1,0:T(8,128)(2,1)S(1)}, u32[]{:S(2)}, u32[]{:S(2)}) %all-to-all-start.1) | async-done | bytes 1572896 | tf_op jit(solution)/shard_map/all_to_all | solution.py:268
  51.5 10.7 %all-to-all-start.2 = ((bf16[16,64,128]{2,1,0:T(8,128)(2,1)}), bf16[16,64,128]{2,1,0:T(8,128)(2,1)S(1)}, u32[]{:S(2)}, u32[]{:S(2)}) async-start(bf16[16,64,128]{2,1,0:T(8,128)(2,1)} %bitcast.15), calls=%async_computation.2 | async-start | bytes 524288 | tf_op jit(solution)/shard_map/all_to_all | solution.py:268
  62.2 0.2 collective-permute-start.3
  62.4 11.4 %all-to-all-done.2 = bf16[16,64,128]{2,1,0:T(8,128)(2,1)S(1)} async-done(((bf16[16,64,128]{2,1,0:T(8,128)(2,1)}), bf16[16,64,128]{2,1,0:T(8,128)(2,1)S(1)}, u32[]{:S(2)}, u32[]{:S(2)}) %all-to-all-start.2) | async-done | bytes 262176 | tf_op jit(solution)/shard_map/all_to_all | solution.py:268
  73.8 16.6 %all_gather.3 = bf16[1024,128]{1,0:T(8,128)(2,1)} all-gather(bf16[64,128]{1,0:T(8,128)(2,1)S(1)} %reduce_sum.42), channel_id=1, replica_groups=mesh['head'=16,'qblk'=16] {'qblk'}, dimensions={0}, use_global_device_ids=true | all-gather | bytes 278528 | tf_op jit(solution)/shard_map/all_gather | solution.py:290
  90.4 15.2 %attend.1 = bf16[2048,256]{1,0:T(8,128)(2,1)} custom-call(s32[40]{0:T(128)} %concatenate.3.tab, bf16[16,3,128,128]{3,2,1,0:T(8,128)(2,1)} %copy-done.2, bf16[16,128,128]{2,1,0:T(8,128)(2,1)} %collective-permute-done.1.v2, bf16[16,2,128,128]{3,2,1,0:T(8,128)(2,1)} %copy-done.1, bf16[16,2,128,128]{3,2,1,0:T(8,128)(2,1)} %collective-permute-done.2.swp, ...), custom_call_target="tpu_custom_call" | custom-call | flops 2000000000 | bytes 6000000 | tf_op jit(solution)/shard_map/attend/pallas_call | solution.py:165
  105.6 19.5 %all_to_all.34 = bf16[16,128,256]{2,1,0:T(8,128)(2,1)S(1)} all-to-all(bf16[16,128,256]{2,1,0:T(8,128)(2,1)} %bitcast.16), channel_id=1, replica_groups=mesh['head'=16,'qblk'=16] {'head'}, dimensions={0} | all-to-all | bytes 2097152 | tf_op jit(solution)/shard_map/all_to_all | solution.py:294
  125.1 1.1 copy.26
  (28 shorter events, 1.0 us)
Async XLA Ops:
  0.0 31.5 %copy-start = (s32[32,8]{0,1:T(8,128)S(1)}, s32[32,8]{0,1:T(8,128)}, u32[]{:S(2)}) copy-start(s32[32,8]{0,1:T(8,128)} %param.9) | copy-start | bytes 3076
  0.0 9.8 %copy-start.3 = (bf16[128,1024]{1,0:T(8,128)(2,1)S(1)}, bf16[128,1024]{1,0:T(8,128)(2,1)}, u32[]{:S(2)}) copy-start(bf16[128,1024]{1,0:T(8,128)(2,1)} %k.1) | copy-start | bytes 786436
  0.0 11.5 %copy-start.5 = (s32[32,5]{0,1:T(8,128)S(1)}, s32[32,5]{0,1:T(8,128)}, u32[]{:S(2)}) copy-start(s32[32,5]{0,1:T(8,128)} %param.8) | copy-start | bytes 1924
  2.2 23.2 %all-to-all-start = ((bf16[16,2,128,128]{3,2,1,0:T(8,128)(2,1)}), bf16[16,2,128,128]{3,2,1,0:T(8,128)(2,1)S(1)}, u32[]{:S(2)}, u32[]{:S(2)}) async-start(bf16[16,2,128,128]{3,2,1,0:T(8,128)(2,1)} %pair.1), calls=%async_computation | async-start | bytes 2097152 | tf_op jit(solution)/shard_map/all_to_all | solution.py:268
  9.8 11.4 %collective-permute-start = (bf16[128,1024]{1,0:T(8,128)(2,1)S(1)}, bf16[128,1024]{1,0:T(8,128)(2,1)S(1)}, u32[]{:S(2)}, u32[]{:S(2)}) collective-permute-start(bf16[128,1024]{1,0:T(8,128)(2,1)S(1)} %copy-done.3), channel_id=1, source_target_pairs={{0,2},{1,3},{2,4},{3,5},{4,6},{5,7},{6,8},{7,9},{8,10},{9,11},{10,... | collective-permute-start | bytes 786440 | tf_op jit(solution)/shard_map/ppermute | solution.py:280
  21.2 0.7 copy-start.4
  25.4 7.4 %copy-start.1 = (bf16[16,2,128,128]{3,2,1,0:T(8,128)(2,1)}, bf16[16,2,128,128]{3,2,1,0:T(8,128)(2,1)S(1)}, u32[]{:S(2)}) copy-start(bf16[16,2,128,128]{3,2,1,0:T(8,128)(2,1)S(1)} %all-to-all-done.kv.own) | copy-start | bytes 3145732
  25.4 26.0 %all-to-all-start.1 = ((bf16[16,3,128,128]{3,2,1,0:T(8,128)(2,1)}), bf16[16,3,128,128]{3,2,1,0:T(8,128)(2,1)S(1)}, u32[]{:S(2)}, u32[]{:S(2)}) async-start(bf16[16,3,128,128]{3,2,1,0:T(8,128)(2,1)} %pack.1), calls=%async_computation.1 | async-start | bytes 3145728 | tf_op jit(solution)/shard_map/all_to_all | solution.py:268
  32.7 13.6 %collective-permute-start.1 = (bf16[16,128,128]{2,1,0:T(8,128)(2,1)S(1)}, bf16[16,128,128]{2,1,0:T(8,128)(2,1)}, u32[]{:S(2)}, u32[]{:S(2)}) collective-permute-start(bf16[16,128,128]{2,1,0:T(8,128)(2,1)S(1)} %slice_bitcast_fusion.1), channel_id=1, source_target_pairs={{0,2},{1,3},{2,4},{3,5},{4,6},{5,7},{6,8},{7,9},{8,10},{9,11},{10,... | collective-permute-start | bytes 1572872 | tf_op jit(solution)/shard_map/ppermute | solution.py:286
  32.8 57.5 %collective-permute-start.2 = (bf16[16,2,128,128]{3,2,1,0:T(8,128)(2,1)S(1)}, bf16[16,2,128,128]{3,2,1,0:T(8,128)(2,1)}, u32[]{:S(2)}, u32[]{:S(2)}) collective-permute-start(bf16[16,2,128,128]{3,2,1,0:T(8,128)(2,1)S(1)} %all-to-all-done.kv.own), channel_id=1, source_target_pairs={{0,1},{1,0},{2,3},{3,2},{4,5},{5,4},{6,7},{7,6},{8,9},{9,8},{10,11... | collective-permute-start | bytes 3145736 | tf_op jit(solution)/shard_map/ppermute | solution.py:287
  46.3 44.0 %collective-permute-start.4 = (bf16[16,128,128]{2,1,0:T(8,128)(2,1)}, bf16[16,128,128]{2,1,0:T(8,128)(2,1)}, u32[]{:S(2)}, u32[]{:S(2)}) collective-permute-start(bf16[16,128,128]{2,1,0:T(8,128)(2,1)} %collective-permute-done.1.v2), channel_id=1, source_target_pairs={{0,1},{1,0},{2,3},{3,2},{4,5},{5,4},{6,7},{7,6},{8,9},{9,8},{10,11... | collective-permute-start | bytes 1572872 | tf_op jit(solution)/shard_map/ppermute | solution.py:288
  51.4 38.9 %copy-start.2 = (bf16[16,3,128,128]{3,2,1,0:T(8,128)(2,1)}, bf16[16,3,128,128]{3,2,1,0:T(8,128)(2,1)S(1)}, u32[]{:S(2)}) copy-start(bf16[16,3,128,128]{3,2,1,0:T(8,128)(2,1)S(1)} %all-to-all-done.1.qk2) | copy-start | bytes 4718596
  51.5 22.3 %all-to-all-start.2 = ((bf16[16,64,128]{2,1,0:T(8,128)(2,1)}), bf16[16,64,128]{2,1,0:T(8,128)(2,1)S(1)}, u32[]{:S(2)}, u32[]{:S(2)}) async-start(bf16[16,64,128]{2,1,0:T(8,128)(2,1)} %bitcast.15), calls=%async_computation.2 | async-start | bytes 524288 | tf_op jit(solution)/shard_map/all_to_all | solution.py:268
  62.2 28.2 %collective-permute-start.3 = (bf16[16,128,128]{2,1,0:T(8,128)(2,1)S(1)}, bf16[16,128,128]{2,1,0:T(8,128)(2,1)}, u32[]{:S(2)}, u32[]{:S(2)}) collective-permute-start(bf16[16,128,128]{2,1,0:T(8,128)(2,1)S(1)} %slice_bitcast_fusion), channel_id=1, source_target_pairs={{0,1},{1,0},{2,3},{3,2},{4,5},{5,4},{6,7},{7,6},{8,9},{9,8},{10,11... | collective-permute-start | bytes 1572872 | tf_op jit(solution)/shard_map/ppermute | solution.py:292
